TPU v7x, 32 devices: a whole 2x2x4 slice. The times are simulated.
32 devices in a mesh: groups: 2 (over x), row: 16 (over z, y, core).
Axes of the slice: x: 2, y: 2, z: 4, core: 2. Of those that a mesh axis runs over, the one named last changes fastest.
Arguments:
- factor_panel: bfloat16 [32768, 2048], P(('groups', 'row')), parts along dimension 0, may hold values from -0.25 to 0.25
- pivots: float32 [4096], P('groups'), parts along dimension 0, may hold values from 1 to 1.25
- right_sides: float32 [32768, 256], P(('groups', 'row')), parts along dimension 0, may hold values from -6 to 6
- block_home: int32 [32], replicated, may hold values from 0 to 31, each once
Outputs:
- remainder: float32 [32768, 256], P('groups', 'row'), parts along dimension 0
- psf_variance: float32 [512], P(('groups', 'row')), parts along dimension 0
There are 2 independent parts, one for each index of `groups`. A program takes and returns all parts, laid end to end along the dimension named above; an argument that names none is the same for every part. Nothing has to cross between parts.
Inputs may be any that keep to these rules, and one draw needn't show every extreme that they name: block_home[g] is the stored position of global block g; position p is slot p % 2 of row device p // 2; every position holds exactly one block.
All inputs are finite; a program needn't handle non-finite values.
Results may differ from a plain program's by a relative error of at most 0.0042.
Values may be sent and summed in bfloat16 or wider, within the bound.
No kernel may reach another device: no remote copies, remote signals or barrier semaphores. Data moves between devices by JAX's collectives and lax.ppermute only.
A program may use at most 128 MiB of HBM per device.

v0:
```python
import jax
import jax.numpy as jnp
from jax import lax
from jax.sharding import PartitionSpec as P

BLOCK = 512
STEPS = 4
PANEL = 2048


def spread(value, axis, source):
    kept = jnp.where(lax.axis_index(axis) == source, value, 0).astype(value.dtype)
    return lax.psum(kept, axis)


def on_device(factor_panel, pivots, right_sides, block_home):
    slot_count = factor_panel.shape[0] // BLOCK
    columns_all = right_sides.shape[1]
    row_count = lax.axis_size("row")
    row_index = lax.axis_index("row")
    block_total = block_home.shape[0]
    positions = row_index * slot_count + jnp.arange(slot_count, dtype=jnp.int32)
    global_ids = jnp.sum(
        jnp.where(
            block_home[None, :] == positions[:, None],
            jnp.arange(block_total, dtype=jnp.int32)[None, :],
            0,
        ),
        axis=1,
    )
    partial_value = right_sides.reshape(slot_count, BLOCK, columns_all)
    factor_blocks = factor_panel.reshape(slot_count, BLOCK, PANEL)
    my_columns = columns_all // row_count
    solutions = []
    for k in range(STEPS):
        slot = block_home[k] % slot_count
        rows = lax.dynamic_index_in_dim(partial_value, slot, 0, keepdims=False)
        diag_slot = block_home[k] % slot_count
        held = lax.dynamic_index_in_dim(factor_blocks, diag_slot, 0, keepdims=False)
        diag_rows = held[:, k * BLOCK : (k + 1) * BLOCK].astype(jnp.float32)
        diag_block = jnp.tril(diag_rows, -1) + jnp.diag(pivots[k * BLOCK : (k + 1) * BLOCK])
        solution = jax.scipy.linalg.solve_triangular(diag_block, rows, lower=True).astype(
            jnp.bfloat16
        )
        solution = spread(solution, "row", block_home[k] // slot_count)
        active = (global_ids > k).astype(jnp.float32)
        product = jnp.einsum(
            "sij,jc->sic",
            factor_blocks[:, :, k * BLOCK : (k + 1) * BLOCK],
            solution,
            preferred_element_type=jnp.float32,
        )
        partial_value = partial_value - active[:, None, None] * product
        partial_value = jnp.where(
            (global_ids == k)[:, None, None], solution.astype(jnp.float32)[None], partial_value
        )
        solutions.append(solution)
    stored = lax.all_to_all(
        partial_value.reshape(slot_count * BLOCK, columns_all),
        "row",
        split_axis=1,
        concat_axis=0,
        tiled=True,
    )
    ordered = jnp.take(stored.reshape(block_total, BLOCK, my_columns), block_home, axis=0)
    remainder = ordered.reshape(block_total * BLOCK, my_columns)
    solved = remainder[: STEPS * BLOCK]
    psf_variance = jnp.mean(solved * solved, axis=0)
    return (remainder, psf_variance)


def solution(mesh):
    in_specs = (P(("groups", "row"), None), P("groups"), P(("groups", "row"), None), P())
    out_specs = (P("groups", "row"), P(("groups", "row")))
    return jax.shard_map(
        on_device, mesh=mesh, in_specs=in_specs, out_specs=out_specs, check_vma=False
    )
```

profile of v0, /device:TPU:9, one launch (start us, length us, event | category | flops | bytes accessed | tf_op | source)
XLA Modules:
  0.0 519.9 jit_solution(8942205453289188810)
XLA Ops:
  7.2 1.4 fusion.108
  16.8 0.8 fusion.107
  17.5 4.6 dynamic-slice_bitcast_fusion.3
  22.1 2.0 fusion.19
  24.1 12.0 %while.8 = (s32[]{:T(128)}, f32[512,512]{1,0:T(8,128)}, s32[4,2]{0,1:T(2,128)S(1)}, f32[4,128,128]{2,1,0:T(8,128)S(1)}, s32[]{:T(128)}) while((s32[]{:T(128)}, f32[512,512]{1,0:T(8,128)}, s32[4,2]{0,1:T(2,128)S(1)}, f32[4,128,128]{2,1,0:T(8,128)S(1)}, s32[]{:T(128)}) %tuple.86), condition=%wide.while_cond, body=%wide.while_body.sunk | while | flops 2 | bytes 131181 | solution.py:42
  24.8 2.3 bitcast_dynamic-update-slice_fusion.8
  27.8 2.3 bitcast_dynamic-update-slice_fusion.8
  30.8 2.3 bitcast_dynamic-update-slice_fusion.8
  33.8 2.2 bitcast_dynamic-update-slice_fusion.8
  36.1 0.7 copy-done.2
  36.8 40.1 %custom-call.6 = f32[4,128,128]{1,2,0:T(8,128)S(1)} custom-call(f32[4,128,128]{2,1,0:T(8,128)} %copy-done.2), custom_call_target="InvertDiagBlocksLowerTriangular" | custom-call | tf_op jit(solution)/shard_map/jit(_solve_triangular)/triangular_solve | solution.py:42
  77.3 1.1 convolution_subtract_fusion.11
  78.8 1.2 convolution_subtract_fusion.7
  80.3 1.3 convolution_subtract_fusion.6
  81.9 0.8 fusion.43
  82.8 1.6 copy.57
  85.1 7.6 %while.9 = (s32[]{:T(128)}, f32[512,512]{1,0:T(8,128)S(1)}, s32[4,2]{0,1:T(2,128)S(1)}, f32[4,128,128]{2,1,0:T(8,128)S(1)}, s32[]{:T(128)}) while((s32[]{:T(128)}, f32[512,512]{1,0:T(8,128)S(1)}, s32[4,2]{0,1:T(2,128)S(1)}, f32[4,128,128]{2,1,0:T(8,128)S(1)}, s32[]{:T(128)}) %tuple.106), condition=%wide.while_cond.clone, body=%wide.while_body.clone.sunk | while | flops 2 | bytes 131181 | solution.py:42
  85.8 1.3 bitcast_dynamic-update-slice_fusion.9
  87.7 1.3 bitcast_dynamic-update-slice_fusion.9
  89.6 1.3 bitcast_dynamic-update-slice_fusion.9
  91.5 1.3 bitcast_dynamic-update-slice_fusion.9
  92.7 0.7 copy-done.3
  93.4 40.2 %custom-call.7 = f32[4,128,128]{1,2,0:T(8,128)S(1)} custom-call(f32[4,128,128]{2,1,0:T(8,128)} %copy-done.3), custom_call_target="InvertDiagBlocksLowerTriangular" | custom-call | tf_op jit(solution)/shard_map/jit(_solve_triangular)/triangular_solve | solution.py:42
  133.7 40.1 %all-reduce.5.cloned.1.call-done = bf16[512,256]{1,0:T(8,128)(2,1)} async-done(((bf16[512,256]{1,0:T(8,128)(2,1)}), bf16[512,256]{1,0:T(8,128)(2,1)}) %all-reduce.5.cloned.1.call-update) | async-done | bytes 262160 | tf_op jit(solution)/shard_map/psum | solution.py:13
  173.7 1.9 copy.55
  175.7 1.9 fusion.11
  178.2 1.1 convolution_subtract_fusion.10
  179.6 1.2 convolution_subtract_fusion.5
  181.1 1.3 convolution_subtract_fusion.4
  182.8 0.7 fusion.42
  183.8 11.1 %while.10 = (s32[]{:T(128)}, f32[512,512]{1,0:T(8,128)}, s32[4,2]{0,1:T(2,128)S(1)}, f32[4,128,128]{2,1,0:T(8,128)S(1)}, s32[]{:T(128)}) while((s32[]{:T(128)}, f32[512,512]{1,0:T(8,128)}, s32[4,2]{0,1:T(2,128)S(1)}, f32[4,128,128]{2,1,0:T(8,128)S(1)}, s32[]{:T(128)}) %tuple.107), condition=%wide.while_cond.clone.1, body=%wide.while_body.clone.1.sunk | while | flops 2 | bytes 131181 | solution.py:42
  184.4 2.2 bitcast_dynamic-update-slice_fusion.10
  187.2 2.2 bitcast_dynamic-update-slice_fusion.10
  190.0 2.2 bitcast_dynamic-update-slice_fusion.10
  192.8 2.1 bitcast_dynamic-update-slice_fusion.10
  195.5 39.3 %custom-call.8 = f32[4,128,128]{1,2,0:T(8,128)S(1)} custom-call(f32[4,128,128]{2,1,0:T(8,128)S(1)} %get-tuple-element.31), custom_call_target="InvertDiagBlocksLowerTriangular" | custom-call | tf_op jit(solution)/shard_map/jit(_solve_triangular)/triangular_solve | solution.py:42
  234.9 39.7 %all-reduce.7.cloned.1.call-done = bf16[512,256]{1,0:T(8,128)(2,1)} async-done(((bf16[512,256]{1,0:T(8,128)(2,1)}), bf16[512,256]{1,0:T(8,128)(2,1)}) %all-reduce.7.cloned.1.call-update) | async-done | bytes 262160 | tf_op jit(solution)/shard_map/psum | solution.py:13
  274.6 1.9 copy.59
  276.4 1.9 fusion.8
  279.0 1.1 convolution_subtract_fusion.9
  280.4 1.2 convolution_subtract_fusion.3
  281.9 1.3 convolution_subtract_fusion.2
  283.5 0.7 fusion.41
  284.4 8.3 %while.11 = (s32[]{:T(128)}, f32[512,512]{1,0:T(8,128)S(1)}, s32[4,2]{0,1:T(2,128)S(1)}, f32[4,128,128]{2,1,0:T(8,128)S(1)}, s32[]{:T(128)}) while((s32[]{:T(128)}, f32[512,512]{1,0:T(8,128)S(1)}, s32[4,2]{0,1:T(2,128)S(1)}, f32[4,128,128]{2,1,0:T(8,128)S(1)}, s32[]{:T(128)}) %tuple.108), condition=%wide.while_cond.clone.2, body=%wide.while_body.clone.2.sunk | while | flops 2 | bytes 131181 | solution.py:42
  285.1 1.4 bitcast_dynamic-update-slice_fusion.11
  287.1 1.4 bitcast_dynamic-update-slice_fusion.11
  289.2 1.4 bitcast_dynamic-update-slice_fusion.11
  291.3 1.4 bitcast_dynamic-update-slice_fusion.11
  293.4 39.3 %custom-call.9 = f32[4,128,128]{1,2,0:T(8,128)S(1)} custom-call(f32[4,128,128]{2,1,0:T(8,128)S(1)} %get-tuple-element.32), custom_call_target="InvertDiagBlocksLowerTriangular" | custom-call | tf_op jit(solution)/shard_map/jit(_solve_triangular)/triangular_solve | solution.py:42
  332.7 42.4 %all-reduce.9.cloned.1.call-done = bf16[512,256]{1,0:T(8,128)(2,1)} async-done(((bf16[512,256]{1,0:T(8,128)(2,1)}), bf16[512,256]{1,0:T(8,128)(2,1)}) %all-reduce.9.cloned.1.call-update) | async-done | bytes 262160 | tf_op jit(solution)/shard_map/psum | solution.py:13
  375.1 1.9 copy.62
  377.0 1.9 fusion.5
  381.4 0.7 fusion.40
  382.2 90.3 %all-reduce.11.cloned.1.call-done = bf16[512,256]{1,0:T(8,128)(2,1)} async-done(((bf16[512,256]{1,0:T(8,128)(2,1)}), bf16[512,256]{1,0:T(8,128)(2,1)}) %all-reduce.11.cloned.1.call-update) | async-done | bytes 262160 | tf_op jit(solution)/shard_map/psum | solution.py:13
  472.5 1.1 copy.65
  473.6 1.8 fusion.2
  475.4 0.8 copy.67
  476.2 1.9 all_to_all.12
  478.1 6.5 %all-to-all-start = ((f32[1024,16,16]{0,2,1:T(8,128)}), f32[1024,16,16]{0,2,1:T(8,128)S(1)}, u32[]{:S(2)}, u32[]{:S(2)}) async-start(f32[1024,16,16]{0,2,1:T(8,128)} %all_to_all.12), calls=%async_computation | async-start | bytes 2097152 | tf_op jit(solution)/shard_map/all_to_all | solution.py:58
  484.7 24.8 %all-to-all-done = f32[1024,16,16]{0,2,1:T(8,128)S(1)} async-done(((f32[1024,16,16]{0,2,1:T(8,128)}), f32[1024,16,16]{0,2,1:T(8,128)S(1)}, u32[]{:S(2)}, u32[]{:S(2)}) %all-to-all-start) | async-done | bytes 1048608 | tf_op jit(solution)/shard_map/all_to_all | solution.py:58
  509.5 0.6 copy.68
  510.3 0.6 copy.69
  510.9 0.6 gather_fusion
  512.3 1.1 broadcast_select_fusion
  (93 shorter events, 18.7 us)
Async XLA Ops:
  7.2 166.6 %all-reduce.5.cloned.1.call-start = ((), (), s32[]{:S(2)}) async-start(), calls=%async_computation.1 | async-start | bytes 524288 | tf_op jit(solution)/shard_map/psum | solution.py:13
  22.1 54.9 %copy-start.1 = (f32[1024,256]{1,0:T(8,128)S(1)}, f32[1024,256]{1,0:T(8,128)}, u32[]{:S(2)}) copy-start(f32[1024,256]{1,0:T(8,128)} %param.8) | copy-start | bytes 3145732
  24.1 60.8 %copy-start.4 = (s32[32]{0:T(128)S(1)}, s32[32]{0:T(128)}, u32[]{:S(2)}) copy-start(s32[32]{0:T(128)} %param.9) | copy-start | bytes 388
  36.1 0.7 copy-start.2
  82.7 191.8 %all-reduce.7.cloned.1.call-start = ((), (), s32[]{:S(2)}) async-start(), calls=%async_computation.2 | async-start | bytes 524288 | tf_op jit(solution)/shard_map/psum | solution.py:13
  92.7 0.7 copy-start.3
  93.4 82.2 %copy-start = (f32[512,512]{1,0:T(8,128)}, f32[512,512]{1,0:T(8,128)S(1)}, u32[]{:S(2)}) copy-start(f32[512,512]{1,0:T(8,128)S(1)} %get-tuple-element.280) | copy-start | bytes 3145732
  183.5 191.6 %all-reduce.9.cloned.1.call-start = ((), (), s32[]{:S(2)}) async-start(), calls=%async_computation.3 | async-start | bytes 524288 | tf_op jit(solution)/shard_map/psum | solution.py:13
  284.3 188.2 %all-reduce.11.cloned.1.call-start = ((), (), s32[]{:S(2)}) async-start(), calls=%async_computation.4 | async-start | bytes 524288 | tf_op jit(solution)/shard_map/psum | solution.py:13
  478.1 31.4 %all-to-all-start = ((f32[1024,16,16]{0,2,1:T(8,128)}), f32[1024,16,16]{0,2,1:T(8,128)S(1)}, u32[]{:S(2)}, u32[]{:S(2)}) async-start(f32[1024,16,16]{0,2,1:T(8,128)} %all_to_all.12), calls=%async_computation | async-start | bytes 2097152 | tf_op jit(solution)/shard_map/all_to_all | solution.py:58
Sparse Core Ops, SparseCore 0:
  82.8 90.8 all-reduce.4
  183.6 90.8 all-reduce.6
  284.4 90.6 all-reduce.8
  382.3 90.1 all-reduce.10
where the time goes:
time: 521 us; the launch traced here: 520 us
  waiting for transfers between devices  237 us (45%)
  other arithmetic  166 us (32%)
  local copies, waits for them, and re-layouts  60.9 us (12%)
  between operations  24.4 us (5%)
  matrix products  24.3 us (5%)
  starting transfers between devices  6.81 us (1%)
    psum x4, waiting for transfers between devices, spread(): return lax.psum(kept, axis)  212 us
    another operation x6, other arithmetic, on_device(): jax.scipy.linalg.solve_triangular(diag_block, rows, lower=True)  161 us
    another operation x53, local copies, waits for them, and re-layouts, on_device(): jax.scipy.linalg.solve_triangular(diag_block, rows, lower=True)  38.8 us
    all_to_all x1, waiting for transfers between devices, on_device(): lax.all_to_all(partial_value.reshape(slot_count * BLOCK, columns_all), 'r...  24.8 us
    another operation x28, matrix products, on_device(): jax.scipy.linalg.solve_triangular(diag_block, rows, lower=True)  16.7 us
  transfers between devices with their start and end apart: 5, of which 5 were waited for; matrix products, arithmetic and copies ran while one was open for 28% of the time, Pallas kernels for 0%

commit v1 on v0

--- a/solution.py
+++ b/solution.py
@@ -6,6 +6,13 @@
 BLOCK = 512
 STEPS = 4
 PANEL = 2048
+
+
+def _rest_corner(base_x):
+    r2 = jnp.split(base_x, lax.axis_size("row"), axis=1)
+    u1 = lax.all_to_all(jnp.stack(r2), "row", split_axis=0, concat_axis=0)
+    oldest = jnp.concatenate(u1, axis=0)
+    return oldest
 
 
 def spread(value, axis, source):
@@ -55,13 +62,7 @@
             (global_ids == k)[:, None, None], solution.astype(jnp.float32)[None], partial_value
         )
         solutions.append(solution)
-    stored = lax.all_to_all(
-        partial_value.reshape(slot_count * BLOCK, columns_all),
-        "row",
-        split_axis=1,
-        concat_axis=0,
-        tiled=True,
-    )
+    stored = _rest_corner(partial_value.reshape(slot_count * BLOCK, columns_all))
     ordered = jnp.take(stored.reshape(block_total, BLOCK, my_columns), block_home, axis=0)
     remainder = ordered.reshape(block_total * BLOCK, my_columns)
     solved = remainder[: STEPS * BLOCK]

time: 521 us -> 554 us (1.063)
  local copies, waits for them, and re-layouts: 60.9 us -> 93.1 us
    another operation x0 -> x20, local copies, waits for them, and re-layouts: none -> 21.7 us  [the longest x18 21 us: _rest_corner(): u1 = lax.all_to_all(jnp.stack(r2), 'row', split_axis=0, concat_axis=0)]
    unnamed x12 -> x31, local copies, waits for them, and re-layouts: 1.53 us -> 14.4 us
  transfers between devices with their start and end apart: 5 -> 5, of which waited for: 5 -> 5; matrix products, arithmetic and copies ran while one was open for 28% -> 27% of each run, Pallas kernels for 0% -> 0%
where the time goes in v1:
time: 554 us; the launch traced here: 551 us
  waiting for transfers between devices  237 us (43%)
  other arithmetic  166 us (30%)
  local copies, waits for them, and re-layouts  93.1 us (17%)
  between operations  24.4 us (4%)
  matrix products  24.3 us (4%)
  starting transfers between devices  6.81 us (1%)
    psum x4, waiting for transfers between devices, spread(): return lax.psum(kept, axis)  212 us
    another operation x6, other arithmetic, on_device(): jax.scipy.linalg.solve_triangular(diag_block, rows, lower=True)  161 us
    another operation x53, local copies, waits for them, and re-layouts, on_device(): jax.scipy.linalg.solve_triangular(diag_block, rows, lower=True)  39.5 us
    all_to_all x1, waiting for transfers between devices, _rest_corner(): u1 = lax.all_to_all(jnp.stack(r2), 'row', split_axis=0, concat_axis=0)  24.8 us
    another operation x18, local copies, waits for them, and re-layouts, _rest_corner(): u1 = lax.all_to_all(jnp.stack(r2), 'row', split_axis=0, concat_axis=0)  21 us
    another operation x28, matrix products, on_device(): jax.scipy.linalg.solve_triangular(diag_block, rows, lower=True)  16.7 us
    unnamed x31, local copies, waits for them, and re-layouts  14.4 us
  transfers between devices with their start and end apart: 5, of which 5 were waited for; matrix products, arithmetic and copies ran while one was open for 27% of the time, Pallas kernels for 0%

profile of v1, /device:TPU:9, one launch (start us, length us, event | category | flops | bytes accessed | tf_op | source)
XLA Modules:
  0.0 551.5 jit_solution(8728922168695491836)
XLA Ops:
  7.2 1.4 fusion.108
  17.6 4.5 dynamic-slice_bitcast_fusion.3
  22.1 2.0 fusion.19
  24.1 11.9 %while.8 = (s32[]{:T(128)}, f32[512,512]{1,0:T(8,128)}, s32[4,2]{0,1:T(2,128)S(1)}, f32[4,128,128]{2,1,0:T(8,128)S(1)}, s32[]{:T(128)}) while((s32[]{:T(128)}, f32[512,512]{1,0:T(8,128)}, s32[4,2]{0,1:T(2,128)S(1)}, f32[4,128,128]{2,1,0:T(8,128)S(1)}, s32[]{:T(128)}) %tuple.101), condition=%wide.while_cond, body=%wide.while_body.sunk | while | flops 2 | bytes 131181 | solution.py:49
  24.8 2.3 bitcast_dynamic-update-slice_fusion.8
  27.8 2.3 bitcast_dynamic-update-slice_fusion.8
  30.7 2.3 bitcast_dynamic-update-slice_fusion.8
  33.7 2.2 bitcast_dynamic-update-slice_fusion.8
  36.7 40.1 %custom-call.6 = f32[4,128,128]{1,2,0:T(8,128)S(1)} custom-call(f32[4,128,128]{2,1,0:T(8,128)} %copy-done.4), custom_call_target="InvertDiagBlocksLowerTriangular" | custom-call | tf_op jit(solution)/shard_map/jit(_solve_triangular)/triangular_solve | solution.py:49
  78.6 1.2 convolution_subtract_fusion.7
  80.1 1.3 convolution_subtract_fusion.6
  82.6 1.6 copy.87
  85.1 8.1 %while.9 = (s32[]{:T(128)}, f32[512,512]{1,0:T(8,128)S(1)}, s32[4,2]{0,1:T(2,128)S(1)}, f32[4,128,128]{2,1,0:T(8,128)S(1)}, s32[]{:T(128)}) while((s32[]{:T(128)}, f32[512,512]{1,0:T(8,128)S(1)}, s32[4,2]{0,1:T(2,128)S(1)}, f32[4,128,128]{2,1,0:T(8,128)S(1)}, s32[]{:T(128)}) %tuple.121), condition=%wide.while_cond.clone, body=%wide.while_body.clone.sunk | while | flops 2 | bytes 131181 | solution.py:49
  85.7 1.4 bitcast_dynamic-update-slice_fusion.9
  87.8 1.4 bitcast_dynamic-update-slice_fusion.9
  89.8 1.4 bitcast_dynamic-update-slice_fusion.9
  91.8 1.4 bitcast_dynamic-update-slice_fusion.9
  93.9 40.2 %custom-call.7 = f32[4,128,128]{1,2,0:T(8,128)S(1)} custom-call(f32[4,128,128]{2,1,0:T(8,128)} %copy-done.5), custom_call_target="InvertDiagBlocksLowerTriangular" | custom-call | tf_op jit(solution)/shard_map/jit(_solve_triangular)/triangular_solve | solution.py:49
  134.1 39.6 %all-reduce.5.cloned.1.call-done = bf16[512,256]{1,0:T(8,128)(2,1)} async-done(((bf16[512,256]{1,0:T(8,128)(2,1)}), bf16[512,256]{1,0:T(8,128)(2,1)}) %all-reduce.5.cloned.1.call-update) | async-done | bytes 262160 | tf_op jit(solution)/shard_map/psum | solution.py:20
  173.7 1.9 copy.85
  175.6 1.9 fusion.11
  178.2 1.1 convolution_subtract_fusion.10
  179.6 1.2 convolution_subtract_fusion.5
  181.1 1.3 convolution_subtract_fusion.4
  183.8 11.7 %while.10 = (s32[]{:T(128)}, f32[512,512]{1,0:T(8,128)}, s32[4,2]{0,1:T(2,128)S(1)}, f32[4,128,128]{2,1,0:T(8,128)S(1)}, s32[]{:T(128)}) while((s32[]{:T(128)}, f32[512,512]{1,0:T(8,128)}, s32[4,2]{0,1:T(2,128)S(1)}, f32[4,128,128]{2,1,0:T(8,128)S(1)}, s32[]{:T(128)}) %tuple.122), condition=%wide.while_cond.clone.1, body=%wide.while_body.clone.1.sunk | while | flops 2 | bytes 131181 | solution.py:49
  184.4 2.3 bitcast_dynamic-update-slice_fusion.10
  187.4 2.3 bitcast_dynamic-update-slice_fusion.10
  190.3 2.3 bitcast_dynamic-update-slice_fusion.10
  193.3 2.2 bitcast_dynamic-update-slice_fusion.10
  196.0 39.3 %custom-call.8 = f32[4,128,128]{1,2,0:T(8,128)S(1)} custom-call(f32[4,128,128]{2,1,0:T(8,128)S(1)} %get-tuple-element.31), custom_call_target="InvertDiagBlocksLowerTriangular" | custom-call | tf_op jit(solution)/shard_map/jit(_solve_triangular)/triangular_solve | solution.py:49
  235.4 39.2 %all-reduce.7.cloned.1.call-done = bf16[512,256]{1,0:T(8,128)(2,1)} async-done(((bf16[512,256]{1,0:T(8,128)(2,1)}), bf16[512,256]{1,0:T(8,128)(2,1)}) %all-reduce.7.cloned.1.call-update) | async-done | bytes 262160 | tf_op jit(solution)/shard_map/psum | solution.py:20
  274.5 1.9 copy.89
  276.4 1.9 fusion.8
  278.9 1.1 convolution_subtract_fusion.9
  280.3 1.2 convolution_subtract_fusion.3
  281.8 1.3 convolution_subtract_fusion.2
  284.3 8.1 %while.11 = (s32[]{:T(128)}, f32[512,512]{1,0:T(8,128)S(1)}, s32[4,2]{0,1:T(2,128)S(1)}, f32[4,128,128]{2,1,0:T(8,128)S(1)}, s32[]{:T(128)}) while((s32[]{:T(128)}, f32[512,512]{1,0:T(8,128)S(1)}, s32[4,2]{0,1:T(2,128)S(1)}, f32[4,128,128]{2,1,0:T(8,128)S(1)}, s32[]{:T(128)}) %tuple.123), condition=%wide.while_cond.clone.2, body=%wide.while_body.clone.2.sunk | while | flops 2 | bytes 131181 | solution.py:49
  285.0 1.3 bitcast_dynamic-update-slice_fusion.11
  287.0 1.3 bitcast_dynamic-update-slice_fusion.11
  289.0 1.3 bitcast_dynamic-update-slice_fusion.11
  291.1 1.3 bitcast_dynamic-update-slice_fusion.11
  293.1 39.3 %custom-call.9 = f32[4,128,128]{1,2,0:T(8,128)S(1)} custom-call(f32[4,128,128]{2,1,0:T(8,128)S(1)} %get-tuple-element.32), custom_call_target="InvertDiagBlocksLowerTriangular" | custom-call | tf_op jit(solution)/shard_map/jit(_solve_triangular)/triangular_solve | solution.py:49
  332.4 42.6 %all-reduce.9.cloned.1.call-done = bf16[512,256]{1,0:T(8,128)(2,1)} async-done(((bf16[512,256]{1,0:T(8,128)(2,1)}), bf16[512,256]{1,0:T(8,128)(2,1)}) %all-reduce.9.cloned.1.call-update) | async-done | bytes 262160 | tf_op jit(solution)/shard_map/psum | solution.py:20
  375.1 1.9 copy.92
  376.9 1.9 fusion.5
  382.1 90.4 %all-reduce.11.cloned.1.call-done = bf16[512,256]{1,0:T(8,128)(2,1)} async-done(((bf16[512,256]{1,0:T(8,128)(2,1)}), bf16[512,256]{1,0:T(8,128)(2,1)}) %all-reduce.11.cloned.1.call-update) | async-done | bytes 262160 | tf_op jit(solution)/shard_map/psum | solution.py:20
  473.6 1.8 fusion.2
  475.8 4.6 slice_bitcast_fusion
  480.4 1.3 copy.98
  482.3 1.8 copy.99
  484.1 1.8 copy.100
  486.0 1.8 copy.101
  487.8 1.8 copy.102
  489.7 1.2 copy.103
  490.9 1.2 copy.104
  492.1 1.2 copy.105
  493.3 1.2 copy.106
  494.5 1.2 copy.107
  496.8 1.5 constant_dynamic-update-slice_fusion.14
  498.3 1.5 constant_dynamic-update-slice_fusion.13
  499.7 1.5 constant_dynamic-update-slice_fusion.12
  501.2 1.5 constant_dynamic-update-slice_fusion.11
  509.7 6.5 %all-to-all-start = ((f32[16,1024,16]{1,2,0:T(8,128)}), f32[16,1024,16]{1,2,0:T(8,128)S(1)}, u32[]{:S(2)}, u32[]{:S(2)}) async-start(f32[16,1024,16]{1,2,0:T(8,128)} %constant_dynamic-update-slice_fusion), calls=%async_computation | async-start | bytes 2097152 | tf_op jit(solution)/shard_map/all_to_all | solution.py:13
  516.3 24.8 %all-to-all-done = f32[16,1024,16]{1,2,0:T(8,128)S(1)} async-done(((f32[16,1024,16]{1,2,0:T(8,128)}), f32[16,1024,16]{1,2,0:T(8,128)S(1)}, u32[]{:S(2)}, u32[]{:S(2)}) %all-to-all-start) | async-done | bytes 1048608 | tf_op jit(solution)/shard_map/all_to_all | solution.py:13
  (129 shorter events, 38.2 us)
Async XLA Ops:
  7.2 166.6 %all-reduce.5.cloned.1.call-start = ((), (), s32[]{:S(2)}) async-start(), calls=%async_computation.1 | async-start | bytes 524288 | tf_op jit(solution)/shard_map/psum | solution.py:20
  22.1 54.8 %copy-start.1 = (f32[1024,256]{1,0:T(8,128)S(1)}, f32[1024,256]{1,0:T(8,128)}, u32[]{:S(2)}) copy-start(f32[1024,256]{1,0:T(8,128)} %param.8) | copy-start | bytes 3145732
  24.1 60.8 %copy-start.6 = (s32[32]{0:T(128)S(1)}, s32[32]{0:T(128)}, u32[]{:S(2)}) copy-start(s32[32]{0:T(128)} %param.9) | copy-start | bytes 388
  36.0 0.7 copy-start.4
  82.6 191.9 %all-reduce.7.cloned.1.call-start = ((), (), s32[]{:S(2)}) async-start(), calls=%async_computation.2 | async-start | bytes 524288 | tf_op jit(solution)/shard_map/psum | solution.py:20
  93.2 0.7 copy-start.5
  93.9 81.7 %copy-start = (f32[512,512]{1,0:T(8,128)}, f32[512,512]{1,0:T(8,128)S(1)}, u32[]{:S(2)}) copy-start(f32[512,512]{1,0:T(8,128)S(1)} %get-tuple-element.296) | copy-start | bytes 3145732
  183.5 191.5 %all-reduce.9.cloned.1.call-start = ((), (), s32[]{:S(2)}) async-start(), calls=%async_computation.3 | async-start | bytes 524288 | tf_op jit(solution)/shard_map/psum | solution.py:20
  284.2 188.3 %all-reduce.11.cloned.1.call-start = ((), (), s32[]{:S(2)}) async-start(), calls=%async_computation.4 | async-start | bytes 524288 | tf_op jit(solution)/shard_map/psum | solution.py:20
  480.4 15.4 %copy-start.3 = (f32[1,1024,16]{2,1,0:T(8,128)S(1)}, f32[1,1024,16]{2,1,0:T(8,128)}, u32[]{:S(2)}) copy-start(f32[1,1024,16]{2,1,0:T(8,128)} %get-tuple-element.82) | copy-start | bytes 196612
  480.4 15.5 %copy-start.2 = (f32[1,1024,16]{2,1,0:T(8,128)S(1)}, f32[1,1024,16]{2,1,0:T(8,128)}, u32[]{:S(2)}) copy-start(f32[1,1024,16]{2,1,0:T(8,128)} %get-tuple-element.81) | copy-start | bytes 196612
  509.7 31.4 %all-to-all-start = ((f32[16,1024,16]{1,2,0:T(8,128)}), f32[16,1024,16]{1,2,0:T(8,128)S(1)}, u32[]{:S(2)}, u32[]{:S(2)}) async-start(f32[16,1024,16]{1,2,0:T(8,128)} %constant_dynamic-update-slice_fusion), calls=%async_computation | async-start | bytes 2097152 | tf_op jit(solution)/shard_map/all_to_all | solution.py:13
Sparse Core Ops, SparseCore 0:
  82.7 90.9 all-reduce.4
  183.6 90.8 all-reduce.6
  284.4 90.6 all-reduce.8
  382.2 90.2 all-reduce.10
